TPU v7x, 32 devices: a whole 2x2x4 slice. The times are simulated.
32 devices in a mesh: groups: 2 (over x), expert: 16 (over z, y, core).
Axes of the slice: x: 2, y: 2, z: 4, core: 2. Of those that a mesh axis runs over, the one named last changes fastest.
Arguments:
- tokens: bfloat16 [2048, 2048], P(('groups', 'expert')), parts along dimension 0, may hold values from -6 to 6
- expert_ids: int32 [2048, 8], P(('groups', 'expert')), parts along dimension 0, may hold values from 0 to 15, as said below
- gate_weights: float32 [2048, 8], P(('groups', 'expert')), parts along dimension 0, may hold values from 0.05 to 0.5
- w_gate: bfloat16 [16, 2048, 768], P('expert'), may hold values from -0.125 to 0.125
- w_up: bfloat16 [16, 2048, 768], P('expert'), may hold values from -0.125 to 0.125
- w_down: bfloat16 [16, 768, 2048], P('expert'), may hold values from -0.21875 to 0.21875
Outputs:
- mixed: bfloat16 [2048, 2048], P(('groups', 'expert')), parts along dimension 0
There are 2 independent parts, one for each index of `groups`. A program takes and returns all parts, laid end to end along the dimension named above; an argument that names none is the same for every part. Nothing has to cross between parts.
Inputs may be any that keep to these rules, and one draw needn't show every extreme that they name: `expert_ids`: each token names 8 different experts. Exactly 2 experts are named exactly 64 times by the tokens of every device; every other expert is named at most 28 times by the tokens of one device, and in every draw some such expert is named exactly 28 times by the tokens of every device.
All inputs are finite; a program needn't handle non-finite values.
Results may differ from a plain program's by a relative error of at most 0.0057.
Values may be sent and summed in bfloat16 or wider, within the bound.
A program may use at most 128 MiB of HBM per device.

v0:
```python
import jax
import jax.numpy as jnp
from jax import lax
from jax.sharding import PartitionSpec as P

row_block = 256


def swiglu_rows(rows_in, weights):
    gate_part = jnp.dot(rows_in, weights[0], preferred_element_type=jnp.float32)
    up_part = jnp.dot(rows_in, weights[1], preferred_element_type=jnp.float32)
    hidden = (jax.nn.silu(gate_part) * up_part).astype(jnp.bfloat16)
    return jnp.dot(hidden, weights[2], preferred_element_type=jnp.float32).astype(jnp.bfloat16)


def run_blocks(source_rows, block_total, weights, results):

    def block_step(block_num, current):
        row_start = block_num * row_block
        rows_in = lax.dynamic_slice_in_dim(source_rows, row_start, row_block, 0)
        return lax.dynamic_update_slice_in_dim(current, swiglu_rows(rows_in, weights), row_start, 0)

    return lax.fori_loop(jnp.zeros((), jnp.int32), block_total, block_step, results)


def route_and_run(tokens, flat_ids, slot_rank, routed, capacity, device_count, own_weights):
    local_tokens, model_width = tokens.shape
    slot_total = flat_ids.shape[0]
    top_count = slot_total // local_tokens
    buffer_rows = device_count * capacity
    padded_rows = (buffer_rows + row_block - 1) // row_block * row_block
    send_slot = jnp.where(routed, flat_ids * capacity + slot_rank, buffer_rows)
    token_of_slot = jnp.arange(slot_total, dtype=jnp.int32) // top_count
    source_row = jnp.zeros((buffer_rows,), jnp.int32).at[send_slot].set(token_of_slot, mode="drop")
    slot_filled = jnp.zeros((buffer_rows,), jnp.int32).at[send_slot].set(1, mode="drop")
    send_counts = jnp.sum(slot_filled.reshape(device_count, capacity), axis=1)
    outgoing = jnp.where(slot_filled[:, None] > 0, tokens[source_row], jnp.zeros((), jnp.bfloat16))
    outgoing = outgoing.reshape(device_count, capacity, model_width)
    count_column = send_counts.astype(jnp.bfloat16).reshape(device_count, 1)
    incoming, arrived = (
        lax.all_to_all(outgoing, "expert", split_axis=0, concat_axis=0, tiled=True),
        lax.all_to_all(count_column, "expert", split_axis=0, concat_axis=0, tiled=True),
    )
    arrived_counts = arrived.reshape(-1).astype(jnp.int32)
    offsets = jnp.cumsum(arrived_counts) - arrived_counts
    live_total = jnp.sum(arrived_counts)
    slot_index = jnp.arange(buffer_rows, dtype=jnp.int32)
    source_of = slot_index // capacity
    within = slot_index % capacity
    is_live = within < arrived_counts[source_of]
    packed_pos = offsets[source_of] + within
    target_pos = jnp.where(is_live, packed_pos, padded_rows)
    compact_source = (
        jnp.full((padded_rows,), buffer_rows, jnp.int32).at[target_pos].set(slot_index, mode="drop")
    )
    flat_incoming = jnp.concatenate(
        [incoming.reshape(buffer_rows, model_width), jnp.zeros((1, model_width), jnp.bfloat16)],
        axis=0,
    )
    compact = flat_incoming[compact_source]
    block_need = (live_total + row_block - 1) // row_block
    results = run_blocks(
        compact, block_need, own_weights, jnp.zeros((padded_rows, model_width), jnp.bfloat16)
    )
    back_slots = results[jnp.where(is_live, packed_pos, 0)]
    back_slots = jnp.where(is_live[:, None], back_slots, jnp.zeros((), jnp.bfloat16))
    back_slots = back_slots.reshape(device_count, capacity, model_width)
    returned_rows = lax.all_to_all(back_slots, "expert", split_axis=0, concat_axis=0, tiled=True)
    picked = returned_rows.reshape(buffer_rows, model_width)[jnp.where(routed, send_slot, 0)]
    return jnp.where(routed[:, None], picked, jnp.zeros((), jnp.bfloat16))


def shards(tokens, expert_ids, gate_weights, w_gate, w_up, w_down):
    device_count = lax.axis_size("expert")
    local_tokens, model_width = tokens.shape
    top_count = expert_ids.shape[1]
    expert_total = device_count * w_gate.shape[0]
    capacity = min(
        local_tokens, 4 * ((local_tokens * top_count + expert_total - 1) // expert_total)
    )
    flat_ids = expert_ids.reshape(-1)
    slot_total = flat_ids.shape[0]
    expert_range = jnp.arange(device_count, dtype=jnp.int32)
    onehot = (flat_ids[:, None] == expert_range[None, :]).astype(jnp.int32)
    slot_rank = jnp.sum(jnp.cumsum(onehot, axis=0) * onehot, axis=1) - 1
    own_weights = (w_gate[0], w_up[0], w_down[0])
    routed = jnp.ones((slot_total,), jnp.bool_)
    slot_values = route_and_run(
        tokens, flat_ids, slot_rank, routed, capacity, device_count, own_weights
    )
    picked = slot_values.reshape(local_tokens, top_count, model_width)
    mixed = jnp.sum(picked.astype(jnp.float32) * gate_weights[:, :, None], axis=1)
    return mixed.astype(jnp.bfloat16)


def solution(mesh):
    placed = (
        P(("groups", "expert"), None),
        P(("groups", "expert"), None),
        P(("groups", "expert"), None),
        P("expert", None, None),
        P("expert", None, None),
        P("expert", None, None),
    )
    return jax.shard_map(
        shards, mesh=mesh, in_specs=placed, out_specs=P(("groups", "expert"), None), check_vma=False
    )
```

profile of v0, /device:TPU:15, one launch (start us, length us, event | category | flops | bytes accessed | tf_op | source)
XLA Modules:
  0.0 305.7 jit_solution(18314291863465316378)
XLA Ops:
  0.0 0.0 copy-start
  0.0 0.8 copy.30
  0.8 0.1 eq.31
  0.9 0.1 eq.27
  1.0 0.7 broadcast_multiply_fusion
  1.7 1.1 reduce-window.19
  2.8 0.2 slice_reduce_fusion
  3.1 0.1 fusion.14
  3.2 0.1 copy.29
  3.3 0.1 mul.40
  3.4 2.4 scatter_custom_fusion
  5.9 0.1 reshape.244
  5.9 0.1 reduce_sum.37
  6.1 0.7 copy.33
  6.8 6.5 %all-to-all-start = ((bf16[16,1,1]{2,1,0:T(2,128)(2,1)}), bf16[16,1,1]{2,1,0:T(2,128)(2,1)S(1)}, u32[]{:S(2)}, u32[]{:S(2)}) async-start(bf16[16,1,1]{2,1,0:T(2,128)(2,1)} %copy.33), calls=%async_computation | async-start | bytes 16384 | tf_op jit(solution)/shard_map/all_to_all | solution.py:42
  13.3 0.1 broadcast_in_dim.61
  13.4 2.4 scatter_custom_fusion.1
  15.9 0.0 copy-done
  15.9 6.0 %gather_fusion = bf16[1024,2048]{1,0:T(8,128)(2,1)} fusion(bf16[64,2048]{1,0:T(8,128)(2,1)S(1)} %copy-done, s32[1024]{0:T(1024)S(1)} %fusion.20), kind=kCustom, calls=%fused_computation | custom fusion | bytes 8392704 | tf_op jit(solution)/shard_map/gather | solution.py:37
  21.9 4.5 %broadcast_select_fusion = bf16[16,64,2048]{2,1,0:T(8,128)(2,1)} fusion(bf16[16,64,2048]{2,1,0:T(8,128)(2,1)} %bitcast.78, pred[16,64]{1,0:T(8,128)(4,1)S(1)} %broadcast_in_dim.61), kind=kLoop, calls=%fused_computation.20 | loop fusion | flops 2097152 | bytes 8389632 | tf_op jit(solution)/shard_map/jit(_where)/select_n | solution.py:37
  26.4 0.0 all-to-all-done
  26.4 6.0 %all-to-all-start.1 = ((bf16[16,64,2048]{2,1,0:T(8,128)(2,1)}), bf16[16,64,2048]{2,1,0:T(8,128)(2,1)}, u32[]{:S(2)}, u32[]{:S(2)}) async-start(bf16[16,64,2048]{2,1,0:T(8,128)(2,1)} %broadcast_select_fusion), calls=%async_computation.1 | async-start | bytes 8388608 | tf_op jit(solution)/shard_map/all_to_all | solution.py:41
  32.7 0.9 convert_reduce_fusion.1
  34.3 0.1 reduce.11
  34.4 0.6 fusion.33
  35.1 4.2 %compare_select_fusion.6 = s32[1024,1]{0,1:T(1,128)S(1)} fusion(s32[]{:T(128)} %bitcast.13, s32[]{:T(128)} %bitcast.14, s32[]{:T(128)} %bitcast.15, s32[]{:T(128)} %bitcast.16, s32[]{:T(128)} %bitcast.17, s32[]{:T(128)} %bitcast.19, s32[]{:T(128)} %bitcast.18), kind=kLoop, calls=%fused_computation.48 | loop fusion | flops 23552 | bytes 4124 | tf_op jit(solution)/shard_map/gather | solution.py:50
  39.3 5.7 %select_select_fusion.1 = s32[1024]{0:T(1024)S(1)} fusion(pred[1024]{0:T(1024)(128)(4,1)S(1)} %compare_reduce_fusion, pred[1024]{0:T(1024)(128)(4,1)S(1)} %compare_reduce_fusion.1, pred[1024]{0:T(1024)(128)(4,1)S(1)} %compare_reduce_fusion.2, pred[1024]{0:T(1024)(128)(4,1)S(1)} %compare_reduce_fusion.3, pred[1024]{0:T(1024)(128)(4,1)S(1)} %compare_reduce_fusion.4, ...), kind=kLoop, calls=%fused_computation.72 | loop fusion | flops 9216 | bytes 17444 | tf_op jit(solution)/shard_map/gather | solution.py:50
  45.0 0.1 gather.29
  45.1 0.7 fusion.34
  45.8 4.5 %compare_select_fusion.7 = s32[1024,1]{0,1:T(1,128)S(1)} fusion(s32[]{:T(128)} %bitcast.34, s32[]{:T(128)} %bitcast.35, s32[]{:T(128)} %bitcast.36, s32[]{:T(128)} %bitcast.37, s32[]{:T(128)} %bitcast.38, s32[]{:T(128)} %bitcast.40, s32[]{:T(128)} %bitcast.39), kind=kLoop, calls=%fused_computation.49 | loop fusion | flops 23552 | bytes 4124 | tf_op jit(solution)/shard_map/gather | solution.py:51
  50.3 5.4 %select_select_fusion = s32[1024]{0:T(1024)S(1)} fusion(pred[1024]{0:T(1024)(128)(4,1)S(1)} %compare_reduce_fusion, pred[1024]{0:T(1024)(128)(4,1)S(1)} %compare_reduce_fusion.1, pred[1024]{0:T(1024)(128)(4,1)S(1)} %compare_reduce_fusion.2, pred[1024]{0:T(1024)(128)(4,1)S(1)} %compare_reduce_fusion.3, pred[1024]{0:T(1024)(128)(4,1)S(1)} %compare_reduce_fusion.4, ...), kind=kLoop, calls=%fused_computation.71 | loop fusion | flops 9216 | bytes 17444 | tf_op jit(solution)/shard_map/gather | solution.py:51
  55.8 4.3 %scatter_custom_fusion.2 = s32[1024]{0:T(1024)S(1)} fusion(s32[1024]{0:T(1024)S(1)} %bitcast.89, s32[1024]{0:T(1024)S(1)} %iota.46, s32[]{:T(128)} %constant.94.clone.1), kind=kCustom, calls=%fused_computation.80 | custom fusion | bytes 4100 | tf_op jit(solution)/shard_map/scatter | solution.py:54
  60.2 64.7 %all-to-all-done.1 = bf16[16,64,2048]{2,1,0:T(8,128)(2,1)} async-done(((bf16[16,64,2048]{2,1,0:T(8,128)(2,1)}), bf16[16,64,2048]{2,1,0:T(8,128)(2,1)}, u32[]{:S(2)}, u32[]{:S(2)}) %all-to-all-start.1) | async-done | bytes 4194336 | tf_op jit(solution)/shard_map/all_to_all | solution.py:41
  124.8 4.7 %concatenate.3 = bf16[1025,2048]{1,0:T(8,128)(2,1)} pad(bf16[1024,2048]{1,0:T(8,128)(2,1)} %bitcast.22, bf16[]{:T(256)} %constant.98.clone.1), padding=0_1x0_0 | pad | bytes 8392706 | tf_op jit(solution)/shard_map/concatenate | solution.py:56
  129.6 11.6 %gather_fusion.1 = bf16[1024,2048]{1,0:T(8,128)(2,1)} fusion(bf16[1025,2048]{1,0:T(8,128)(2,1)} %concatenate.3, s32[1024]{0:T(1024)S(1)} %fusion.21), kind=kCustom, calls=%fused_computation.1 | custom fusion | bytes 8392704 | tf_op jit(solution)/shard_map/gather | solution.py:60
  141.1 0.0 copy-start.2
  141.1 2.5 broadcast_in_dim.60
  143.6 0.4 copy-done.2
  144.0 19.3 %while.10 = (s32[]{:T(128)}, bf16[1024,2048]{1,0:T(8,128)(2,1)}, s32[]{:T(128)}, bf16[1024,2048]{1,0:T(8,128)(2,1)}, bf16[2048,768]{1,0:T(8,128)(2,1)S(1)}, /*in...) while((s32[]{:T(128)}, bf16[1024,2048]{1,0:T(8,128)(2,1)}, ...), condition=%wide.region_10.11_spmd, body=%wide.region_9.10_spmd.sunk | while | flops 2417623040 | bytes 14156959 | solution.py:23
  144.0 3.1 %fusion.50 = f32[256,768]{1,0:T(8,128)} fusion(bf16[2048,768]{1,0:T(8,128)(2,1)S(1)} %get-tuple-element.164, bf16[1024,2048]{1,0:T(8,128)(2,1)} %get-tuple-element.163, s32[]{:T(128)S(6)} %select_n.234), kind=kOutput, calls=%fused_computation.12.clone.1 | convolution fusion | flops 805306368 | bytes 4980740 | tf_op jit(solution)/shard_map/while/body/dot_general | solution.py:10
  147.2 6.6 %fusion.51 = bf16[1024,2048]{1,0:T(8,128)(2,1)} fusion(bf16[1024,2048]{1,0:T(8,128)(2,1)} %get-tuple-element.150, s32[]{:T(128)S(6)} %select_n.234, bf16[768,2048]{1,0:T(8,128)(2,1)} %get-tuple-element.166, bf16[2048,768]{1,0:T(8,128)(2,1)} %get-tuple-element.165, bf16[1024,2048]{1,0:T(8,128)(2,1)} %get-tuple-element.163, f32[256,768]{1,0:T(8,128)} %fusion.50), kind=kOutput, calls=%fused_computation.8.clone.1 | convolution fusion | flops 1612316672 | bytes 9176064 | tf_op jit(solution)/shard_map/while/body/dot_general | solution.py:13
  153.7 3.1 %fusion.50 = f32[256,768]{1,0:T(8,128)} fusion(bf16[2048,768]{1,0:T(8,128)(2,1)S(1)} %get-tuple-element.164, bf16[1024,2048]{1,0:T(8,128)(2,1)} %get-tuple-element.163, s32[]{:T(128)S(6)} %select_n.234), kind=kOutput, calls=%fused_computation.12.clone.1 | convolution fusion | flops 805306368 | bytes 4980740 | tf_op jit(solution)/shard_map/while/body/dot_general | solution.py:10
  156.8 6.5 %fusion.51 = bf16[1024,2048]{1,0:T(8,128)(2,1)} fusion(bf16[1024,2048]{1,0:T(8,128)(2,1)} %get-tuple-element.150, s32[]{:T(128)S(6)} %select_n.234, bf16[768,2048]{1,0:T(8,128)(2,1)} %get-tuple-element.166, bf16[2048,768]{1,0:T(8,128)(2,1)} %get-tuple-element.165, bf16[1024,2048]{1,0:T(8,128)(2,1)} %get-tuple-element.163, f32[256,768]{1,0:T(8,128)} %fusion.50), kind=kOutput, calls=%fused_computation.8.clone.1 | convolution fusion | flops 1612316672 | bytes 9176064 | tf_op jit(solution)/shard_map/while/body/dot_general | solution.py:13
  163.3 11.6 %gather_fusion.2 = bf16[1024,2048]{1,0:T(8,128)(2,1)} fusion(bf16[1024,2048]{1,0:T(8,128)(2,1)} %get-tuple-element.43, s32[1024]{0:T(1024)S(1)} %broadcast_clamp_fusion), kind=kCustom, calls=%fused_computation.2 | custom fusion | bytes 8392704 | tf_op jit(solution)/shard_map/gather | solution.py:65
  174.9 4.5 %broadcast_select_fusion.1 = bf16[16,64,2048]{2,1,0:T(8,128)(2,1)} fusion(bf16[16,64,2048]{2,1,0:T(8,128)(2,1)} %bitcast.77, pred[16,64]{1,0:T(8,128)(4,1)S(1)} %fusion.16), kind=kLoop, calls=%fused_computation.21 | loop fusion | flops 2097152 | bytes 8389632 | tf_op jit(solution)/shard_map/jit(_where)/select_n | solution.py:66
  179.4 0.0 copy-start.1
  179.4 24.2 %all-to-all-start.2 = ((bf16[16,64,2048]{2,1,0:T(8,128)(2,1)}), bf16[16,64,2048]{2,1,0:T(8,128)(2,1)}, u32[]{:S(2)}, u32[]{:S(2)}) async-start(bf16[16,64,2048]{2,1,0:T(8,128)(2,1)} %broadcast_select_fusion.1), calls=%async_computation.2 | async-start | bytes 8388608 | tf_op jit(solution)/shard_map/all_to_all | solution.py:68
  203.6 0.0 copy-done.1
  203.6 0.1 copy.35
  203.7 92.4 %all-to-all-done.2 = bf16[16,64,2048]{2,1,0:T(8,128)(2,1)} async-done(((bf16[16,64,2048]{2,1,0:T(8,128)(2,1)}), bf16[16,64,2048]{2,1,0:T(8,128)(2,1)}, u32[]{:S(2)}, u32[]{:S(2)}) %all-to-all-start.2) | async-done | bytes 4194336 | tf_op jit(solution)/shard_map/all_to_all | solution.py:68
  296.0 7.1 %gather_fusion.3 = bf16[512,2048]{1,0:T(8,128)(2,1)S(1)} fusion(bf16[1024,2048]{1,0:T(8,128)(2,1)} %bitcast.49, s32[1024]{0:T(1024)S(1)} %pad_clamp_fusion), kind=kCustom, calls=%fused_computation.3 | custom fusion | bytes 4196352 | tf_op jit(solution)/shard_map/gather | solution.py:69
  303.2 2.5 fusion.12
  (28 shorter events, 0.5 us)
Async XLA Ops:
  0.0 15.9 %copy-start = (bf16[64,2048]{1,0:T(8,128)(2,1)S(1)}, bf16[64,2048]{1,0:T(8,128)(2,1)}, u32[]{:S(2)}) copy-start(bf16[64,2048]{1,0:T(8,128)(2,1)} %param.8) | copy-start | bytes 786436
  6.8 19.6 %all-to-all-start = ((bf16[16,1,1]{2,1,0:T(2,128)(2,1)}), bf16[16,1,1]{2,1,0:T(2,128)(2,1)S(1)}, u32[]{:S(2)}, u32[]{:S(2)}) async-start(bf16[16,1,1]{2,1,0:T(2,128)(2,1)} %copy.33), calls=%async_computation | async-start | bytes 16384 | tf_op jit(solution)/shard_map/all_to_all | solution.py:42
  26.4 98.5 %all-to-all-start.1 = ((bf16[16,64,2048]{2,1,0:T(8,128)(2,1)}), bf16[16,64,2048]{2,1,0:T(8,128)(2,1)}, u32[]{:S(2)}, u32[]{:S(2)}) async-start(bf16[16,64,2048]{2,1,0:T(8,128)(2,1)} %broadcast_select_fusion), calls=%async_computation.1 | async-start | bytes 8388608 | tf_op jit(solution)/shard_map/all_to_all | solution.py:41
  141.1 2.9 copy-start.2
  179.4 24.2 %copy-start.1 = (f32[64,8]{0,1:T(8,128)S(1)}, f32[64,8]{0,1:T(8,128)}, u32[]{:S(2)}) copy-start(f32[64,8]{0,1:T(8,128)} %param.10) | copy-start | bytes 6148
  179.4 116.6 %all-to-all-start.2 = ((bf16[16,64,2048]{2,1,0:T(8,128)(2,1)}), bf16[16,64,2048]{2,1,0:T(8,128)(2,1)}, u32[]{:S(2)}, u32[]{:S(2)}) async-start(bf16[16,64,2048]{2,1,0:T(8,128)(2,1)} %broadcast_select_fusion.1), calls=%async_computation.2 | async-start | bytes 8388608 | tf_op jit(solution)/shard_map/all_to_all | solution.py:68
where the time goes:
time: 307 us; the launch traced here: 306 us
  waiting for transfers between devices  157 us (51%)
  local copies, waits for them, and re-layouts  56.8 us (19%)
  starting transfers between devices  36.7 us (12%)
  other arithmetic  35 us (11%)
  matrix products  19.3 us (6%)
    all_to_all x1, waiting for transfers between devices, route_and_run(): lax.all_to_all(back_slots, 'expert', split_axis=0, concat_axis=0, tiled=T...  92.4 us
    all_to_all x1, waiting for transfers between devices, route_and_run(): lax.all_to_all(outgoing, 'expert', split_axis=0, concat_axis=0, tiled=True)  64.7 us
    all_to_all x1, starting transfers between devices, route_and_run(): lax.all_to_all(back_slots, 'expert', split_axis=0, concat_axis=0, tiled=T...  24.2 us
    dot_general x2, matrix products, swiglu_rows(): jnp.dot(hidden, weights[2], preferred_element_type=jnp.float32)  13.1 us
    gather x1, local copies, waits for them, and re-layouts, route_and_run(): compact = flat_incoming[compact_source]  11.6 us
    gather x1, local copies, waits for them, and re-layouts, route_and_run(): back_slots = results[jnp.where(is_live, packed_pos, 0)]  11.6 us
    gather x11, other arithmetic, route_and_run(): is_live = within < arrived_counts[source_of]  10.2 us
    gather x2, other arithmetic, route_and_run(): packed_pos = offsets[source_of] + within  9.94 us
  transfers between devices with their start and end apart: 3, of which 2 were waited for; matrix products, arithmetic and copies ran while one was open for 13% of the time, Pallas kernels for 0%

commit v1 on v0

--- a/solution.py
+++ b/solution.py
@@ -4,6 +4,18 @@
 from jax.sharding import PartitionSpec as P
 
 row_block = 256
+
+
+def report_the_vectors(xx, dim_at, frame):
+    aux = xx.shape
+    base_arr = xx.reshape(*aux[:dim_at], frame, aux[dim_at] // frame, *aux[dim_at + 1 :])
+    return jnp.moveaxis(base_arr, dim_at, 0)
+
+
+def report_leaf(local_values, dimension_no):
+    local_part = list(local_values.shape[1:])
+    local_part[dimension_no] *= local_values.shape[0]
+    return jnp.moveaxis(local_values, 0, dimension_no).reshape(local_part)
 
 
 def swiglu_rows(rows_in, weights):
@@ -65,7 +77,22 @@
     back_slots = results[jnp.where(is_live, packed_pos, 0)]
     back_slots = jnp.where(is_live[:, None], back_slots, jnp.zeros((), jnp.bfloat16))
     back_slots = back_slots.reshape(device_count, capacity, model_width)
-    returned_rows = lax.all_to_all(back_slots, "expert", split_axis=0, concat_axis=0, tiled=True)
+
+    def do_lines(field_in, lane_axis, block_in, inputs=0):
+        value_now = lax.axis_size(lane_axis)
+        n_now = lax.axis_index(lane_axis)
+        v1, front = (value_now, n_now)
+        t1 = report_the_vectors(field_in, block_in, v1)
+        vals = [t1[front]]
+        for src_i in range(1, v1):
+            g_now = t1[front ^ src_i]
+            vals.append(
+                lax.ppermute(g_now, axis_name=lane_axis, perm=[(q, q ^ src_i) for q in range(v1)])
+            )
+        t1 = jnp.stack(vals)[front ^ jnp.arange(v1)]
+        return report_leaf(t1, inputs)
+
+    returned_rows = do_lines(back_slots, "expert", 0)
     picked = returned_rows.reshape(buffer_rows, model_width)[jnp.where(routed, send_slot, 0)]
     return jnp.where(routed[:, None], picked, jnp.zeros((), jnp.bfloat16))
 

time: 307 us -> 319 us (1.039)
  waiting for transfers between devices: 157 us -> 134 us
  local copies, waits for them, and re-layouts: 56.8 us -> 74.9 us
  starting transfers between devices: 36.7 us -> 53.7 us
    all_to_all x1 -> x0, waiting for transfers between devices: 92.4 us -> none  [route_and_run(): lax.all_to_all(back_slots, 'expert', split_axis=0, concat_axis=0, tiled=T...]
    ppermute x0 -> x15, waiting for transfers between devices: none -> 69.4 us  [do_lines(): lax.ppermute(g_now, axis_name=lane_axis, perm=[(q, q ^ src_i) for q in ra...]
    ppermute x0 -> x15, starting transfers between devices: none -> 41.1 us  [do_lines(): lax.ppermute(g_now, axis_name=lane_axis, perm=[(q, q ^ src_i) for q in ra...]
    all_to_all x1 -> x0, starting transfers between devices: 24.2 us -> none  [route_and_run(): lax.all_to_all(back_slots, 'expert', split_axis=0, concat_axis=0, tiled=T...]
    unnamed x8 -> x22, local copies, waits for them, and re-layouts: 1.31 us -> 12.5 us
    gather x0 -> x1, local copies, waits for them, and re-layouts: none -> 4.97 us  [do_lines(): t1 = jnp.stack(vals)[front ^ jnp.arange(v1)]]
    gather x2 -> x1, other arithmetic: 9.94 us -> 5.55 us  [route_and_run(): packed_pos = offsets[source_of] + within]
    gather x11 -> x7, other arithmetic: 10.2 us -> 14.4 us  [route_and_run(): is_live = within < arrived_counts[source_of]]
  transfers between devices with their start and end apart: 3 -> 17, of which waited for: 2 -> 9; matrix products, arithmetic and copies ran while one was open for 13% -> 16% of each run, Pallas kernels for 0% -> 0%
where the time goes in v1:
time: 319 us; the launch traced here: 316 us
  waiting for transfers between devices  134 us (42%)
  local copies, waits for them, and re-layouts  74.9 us (23%)
  starting transfers between devices  53.7 us (17%)
  other arithmetic  32.8 us (10%)
  matrix products  19.4 us (6%)
    ppermute x15, waiting for transfers between devices, do_lines(): lax.ppermute(g_now, axis_name=lane_axis, perm=[(q, q ^ src_i) for q in ra...  69.4 us
    all_to_all x1, waiting for transfers between devices, route_and_run(): lax.all_to_all(outgoing, 'expert', split_axis=0, concat_axis=0, tiled=True)  64.9 us
    ppermute x15, starting transfers between devices, do_lines(): lax.ppermute(g_now, axis_name=lane_axis, perm=[(q, q ^ src_i) for q in ra...  41.1 us
    gather x7, other arithmetic, route_and_run(): is_live = within < arrived_counts[source_of]  14.4 us
    dot_general x2, matrix products, swiglu_rows(): jnp.dot(hidden, weights[2], preferred_element_type=jnp.float32)  13.1 us
    unnamed x22, local copies, waits for them, and re-layouts  12.5 us
    gather x1, local copies, waits for them, and re-layouts, route_and_run(): compact = flat_incoming[compact_source]  11.6 us
    gather x1, local copies, waits for them, and re-layouts, route_and_run(): back_slots = results[jnp.where(is_live, packed_pos, 0)]  11.6 us
  transfers between devices with their start and end apart: 17, of which 9 were waited for; matrix products, arithmetic and copies ran while one was open for 16% of the time, Pallas kernels for 0%

profile of v1, /device:TPU:15, one launch (start us, length us, event | category | flops | bytes accessed | tf_op | source)
XLA Modules:
  0.0 315.9 jit_solution(6217946692218486371)
XLA Ops:
  0.0 0.8 copy.30
  1.0 0.7 broadcast_multiply_fusion
  1.7 1.1 reduce-window.19
  3.4 2.4 scatter_custom_fusion
  6.1 0.7 copy.33
  6.8 6.5 %all-to-all-start = ((bf16[16,1,1]{2,1,0:T(2,128)(2,1)}), bf16[16,1,1]{2,1,0:T(2,128)(2,1)S(1)}, u32[]{:S(2)}, u32[]{:S(2)}) async-start(bf16[16,1,1]{2,1,0:T(2,128)(2,1)} %copy.33), calls=%async_computation | async-start | bytes 16384 | tf_op jit(solution)/shard_map/all_to_all | solution.py:54
  13.3 2.4 scatter_custom_fusion.1
  15.9 6.0 %gather_fusion = bf16[1024,2048]{1,0:T(8,128)(2,1)} fusion(bf16[64,2048]{1,0:T(8,128)(2,1)S(1)} %copy-done, s32[1024]{0:T(1024)S(1)} %get-tuple-element.120), kind=kCustom, calls=%fused_computation | custom fusion | bytes 8392704 | tf_op jit(solution)/shard_map/gather | solution.py:49
  21.9 4.5 %broadcast_select_fusion = bf16[16,64,2048]{2,1,0:T(8,128)(2,1)} fusion(bf16[16,64,2048]{2,1,0:T(8,128)(2,1)} %bitcast.142, pred[16,64]{1,0:T(8,128)(4,1)S(1)} %broadcast_in_dim.64), kind=kLoop, calls=%fused_computation.21 | loop fusion | flops 2097152 | bytes 8389632 | tf_op jit(solution)/shard_map/jit(_where)/select_n | solution.py:49
  26.4 6.0 %all-to-all-start.1 = ((bf16[16,64,2048]{2,1,0:T(8,128)(2,1)}), bf16[16,64,2048]{2,1,0:T(8,128)(2,1)}, u32[]{:S(2)}, u32[]{:S(2)}) async-start(bf16[16,64,2048]{2,1,0:T(8,128)(2,1)} %broadcast_select_fusion), calls=%async_computation.1 | async-start | bytes 8388608 | tf_op jit(solution)/shard_map/all_to_all | solution.py:53
  32.5 0.9 convert_reduce_fusion.1
  34.3 0.6 fusion.34
  34.9 0.7 fusion.35
  35.6 8.7 %compare_select_fusion.6 = (s32[1024,1]{0,1:T(1,128)S(1)}, s32[1024,1]{0,1:T(1,128)S(1)}) fusion(s32[]{:T(128)} %bitcast.13, s32[]{:T(128)} %bitcast.14, s32[]{:T(128)} %bitcast.15, s32[]{:T(128)} %bitcast.16, s32[]{:T(128)} %bitcast.17, s32[]{:T(128)} %bitcast.19, s32[]{:T(128)} %bitcast.18, s32[]{:T(128)} %bitcast.40, s32[]{:T(128)} %bitcast.39, ...), kind=kLoop, calls=%fused_computation.80 | loop fusion | flops 29696 | bytes 8248 | tf_op jit(solution)/shard_map/gather | solution.py:62
  44.3 5.6 %select_select_fusion.1 = s32[1024]{0:T(1024)S(1)} fusion(pred[1024]{0:T(1024)(128)(4,1)S(1)} %get-tuple-element.110, pred[1024]{0:T(1024)(128)(4,1)S(1)} %get-tuple-element.111, pred[1024]{0:T(1024)(128)(4,1)S(1)} %get-tuple-element.112, pred[1024]{0:T(1024)(128)(4,1)S(1)} %get-tuple-element.113, pred[1024]{0:T(1024)(128)(4,1)S(1)} %get-tuple-element.114, ...), kind=kLoop, calls=%fused_computation.105 | loop fusion | flops 9216 | bytes 17444 | tf_op jit(solution)/shard_map/gather | solution.py:62
  50.0 5.5 %select_select_fusion = s32[1024]{0:T(1024)S(1)} fusion(pred[1024]{0:T(1024)(128)(4,1)S(1)} %get-tuple-element.110, pred[1024]{0:T(1024)(128)(4,1)S(1)} %get-tuple-element.111, pred[1024]{0:T(1024)(128)(4,1)S(1)} %get-tuple-element.112, pred[1024]{0:T(1024)(128)(4,1)S(1)} %get-tuple-element.113, pred[1024]{0:T(1024)(128)(4,1)S(1)} %get-tuple-element.114, ...), kind=kLoop, calls=%fused_computation.104 | loop fusion | flops 9216 | bytes 17444 | tf_op jit(solution)/shard_map/gather | solution.py:63
  55.5 4.3 %scatter_custom_fusion.2 = s32[1024]{0:T(1024)S(1)} fusion(s32[1024]{0:T(1024)S(1)} %bitcast.154, s32[1024]{0:T(1024)S(1)} %iota.50, s32[]{:T(128)} %constant.113.clone.1), kind=kCustom, calls=%fused_computation.114 | custom fusion | bytes 4100 | tf_op jit(solution)/shard_map/scatter | solution.py:66
  59.9 64.9 %all-to-all-done.1 = bf16[16,64,2048]{2,1,0:T(8,128)(2,1)} async-done(((bf16[16,64,2048]{2,1,0:T(8,128)(2,1)}), bf16[16,64,2048]{2,1,0:T(8,128)(2,1)}, u32[]{:S(2)}, u32[]{:S(2)}) %all-to-all-start.1) | async-done | bytes 4194336 | tf_op jit(solution)/shard_map/all_to_all | solution.py:53
  124.8 4.7 %concatenate.3 = bf16[1025,2048]{1,0:T(8,128)(2,1)} pad(bf16[1024,2048]{1,0:T(8,128)(2,1)} %bitcast.22, bf16[]{:T(256)} %constant.117.clone.1), padding=0_1x0_0 | pad | bytes 8392706 | tf_op jit(solution)/shard_map/concatenate | solution.py:68
  129.6 11.6 %gather_fusion.1 = bf16[1024,2048]{1,0:T(8,128)(2,1)} fusion(bf16[1025,2048]{1,0:T(8,128)(2,1)} %concatenate.3, s32[1024]{0:T(1024)S(1)} %fusion.21), kind=kCustom, calls=%fused_computation.1 | custom fusion | bytes 8392704 | tf_op jit(solution)/shard_map/gather | solution.py:72
  141.1 2.4 broadcast_in_dim.63
  143.6 0.4 copy-done.2
  144.0 19.4 %while.10 = (s32[]{:T(128)}, bf16[1024,2048]{1,0:T(8,128)(2,1)}, s32[]{:T(128)}, bf16[1024,2048]{1,0:T(8,128)(2,1)}, bf16[2048,768]{1,0:T(8,128)(2,1)S(1)}, /*in...) while((s32[]{:T(128)}, bf16[1024,2048]{1,0:T(8,128)(2,1)}, ...), condition=%wide.region_10.11_spmd, body=%wide.region_9.10_spmd.sunk | while | flops 2417623040 | bytes 14156959 | solution.py:35
  144.0 3.1 fusion.51
  147.2 6.5 %fusion.52 = bf16[1024,2048]{1,0:T(8,128)(2,1)} fusion(bf16[1024,2048]{1,0:T(8,128)(2,1)} %get-tuple-element.178, s32[]{:T(128)S(6)} %select_n.318, bf16[768,2048]{1,0:T(8,128)(2,1)} %get-tuple-element.194, bf16[2048,768]{1,0:T(8,128)(2,1)} %get-tuple-element.193, bf16[1024,2048]{1,0:T(8,128)(2,1)} %get-tuple-element.191, f32[256,768]{1,0:T(8,128)} %fusion.51), kind=kOutput, calls=%fused_computation.9.clone.1 | convolution fusion | flops 1612316672 | bytes 9176064 | tf_op jit(solution)/shard_map/while/body/dot_general | solution.py:25
  153.7 3.2 fusion.51
  156.8 6.6 %fusion.52 = bf16[1024,2048]{1,0:T(8,128)(2,1)} fusion(bf16[1024,2048]{1,0:T(8,128)(2,1)} %get-tuple-element.178, s32[]{:T(128)S(6)} %select_n.318, bf16[768,2048]{1,0:T(8,128)(2,1)} %get-tuple-element.194, bf16[2048,768]{1,0:T(8,128)(2,1)} %get-tuple-element.193, bf16[1024,2048]{1,0:T(8,128)(2,1)} %get-tuple-element.191, f32[256,768]{1,0:T(8,128)} %fusion.51), kind=kOutput, calls=%fused_computation.9.clone.1 | convolution fusion | flops 1612316672 | bytes 9176064 | tf_op jit(solution)/shard_map/while/body/dot_general | solution.py:25
  163.4 11.6 %gather_fusion.2 = bf16[1024,2048]{1,0:T(8,128)(2,1)} fusion(bf16[1024,2048]{1,0:T(8,128)(2,1)} %get-tuple-element.43, s32[1024]{0:T(1024)S(1)} %broadcast_clamp_fusion), kind=kCustom, calls=%fused_computation.2 | custom fusion | bytes 8392704 | tf_op jit(solution)/shard_map/gather | solution.py:77
  175.0 2.5 broadcast_select_fusion.1
  177.5 1.3 dynamic-slice_bitcast_fusion
  179.1 2.0 collective-permute-start.2
  181.1 2.8 collective-permute-start.3
  184.3 2.8 collective-permute-start.5
  187.1 1.7 bitcast_dynamic-update-slice_fusion.14
  188.8 4.1 %collective-permute-start.6 = (bf16[1,64,2048]{2,1,0:T(8,128)(2,1)S(1)}, bf16[1,64,2048]{2,1,0:T(8,128)(2,1)S(1)}, u32[]{:S(2)}, u32[]{:S(2)}) collective-permute-start(bf16[1,64,2048]{2,1,0:T(8,128)(2,1)S(1)} %get-tuple-element.68), channel_id=1, source_target_pairs={{0,7},{1,6},{2,5},{3,4},{4,3},{5,2},{6,1},{7,0},{8,15},{9,14},{10,... | collective-permute-start | bytes 786440 | tf_op jit(solution)/shard_map/ppermute | solution.py:90
  192.9 0.7 bitcast_dynamic-update-slice_fusion.13
  193.6 20.1 %collective-permute-start.7 = (bf16[1,64,2048]{2,1,0:T(8,128)(2,1)S(1)}, bf16[1,64,2048]{2,1,0:T(8,128)(2,1)S(1)}, u32[]{:S(2)}, u32[]{:S(2)}) collective-permute-start(bf16[1,64,2048]{2,1,0:T(8,128)(2,1)S(1)} %get-tuple-element.67), channel_id=1, source_target_pairs={{0,8},{1,9},{2,10},{3,11},{4,12},{5,13},{6,14},{7,15},{8,0},{9,1},... | collective-permute-start | bytes 786440 | tf_op jit(solution)/shard_map/ppermute | solution.py:90
  213.7 0.7 bitcast_dynamic-update-slice_fusion.12
  214.4 0.7 bitcast_dynamic-update-slice_fusion.11
  215.1 2.5 collective-permute-start.9
  217.6 0.7 bitcast_dynamic-update-slice_fusion.10
  218.3 4.3 %collective-permute-start.10 = (bf16[1,64,2048]{2,1,0:T(8,128)(2,1)S(1)}, bf16[1,64,2048]{2,1,0:T(8,128)(2,1)S(1)}, u32[]{:S(2)}, u32[]{:S(2)}) collective-permute-start(bf16[1,64,2048]{2,1,0:T(8,128)(2,1)S(1)} %get-tuple-element.64), channel_id=1, source_target_pairs={{0,11},{1,10},{2,9},{3,8},{4,15},{5,14},{6,13},{7,12},{8,3},{9,2},... | collective-permute-start | bytes 786440 | tf_op jit(solution)/shard_map/ppermute | solution.py:90
  222.7 0.7 bitcast_dynamic-update-slice_fusion.9
  223.4 2.0 collective-permute-start.11
  225.3 0.7 bitcast_dynamic-update-slice_fusion.8
  226.1 18.2 %collective-permute-done.7 = bf16[1,64,2048]{2,1,0:T(8,128)(2,1)S(1)} collective-permute-done((bf16[1,64,2048]{2,1,0:T(8,128)(2,1)S(1)}, bf16[1,64,2048]{2,1,0:T(8,128)(2,1)S(1)}, u32[]{:S(2)}, u32[]{:S(2)}) %collective-permute-start.7) | collective-permute-done | bytes 262176 | tf_op jit(solution)/shard_map/ppermute | solution.py:90
  244.3 0.7 bitcast_dynamic-update-slice_fusion.7
  245.1 10.3 %collective-permute-done.8 = bf16[1,64,2048]{2,1,0:T(8,128)(2,1)S(1)} collective-permute-done((bf16[1,64,2048]{2,1,0:T(8,128)(2,1)S(1)}, bf16[1,64,2048]{2,1,0:T(8,128)(2,1)S(1)}, u32[]{:S(2)}, u32[]{:S(2)}) %collective-permute-start.8) | collective-permute-done | bytes 262176 | tf_op jit(solution)/shard_map/ppermute | solution.py:90
  255.4 0.7 bitcast_dynamic-update-slice_fusion.6
  256.1 5.0 %collective-permute-done.9 = bf16[1,64,2048]{2,1,0:T(8,128)(2,1)S(1)} collective-permute-done((bf16[1,64,2048]{2,1,0:T(8,128)(2,1)S(1)}, bf16[1,64,2048]{2,1,0:T(8,128)(2,1)S(1)}, u32[]{:S(2)}, u32[]{:S(2)}) %collective-permute-start.9) | collective-permute-done | bytes 262176 | tf_op jit(solution)/shard_map/ppermute | solution.py:90
  261.2 0.7 bitcast_dynamic-update-slice_fusion.5
  261.9 16.1 %collective-permute-done.10 = bf16[1,64,2048]{2,1,0:T(8,128)(2,1)S(1)} collective-permute-done((bf16[1,64,2048]{2,1,0:T(8,128)(2,1)S(1)}, bf16[1,64,2048]{2,1,0:T(8,128)(2,1)S(1)}, u32[]{:S(2)}, u32[]{:S(2)}) %collective-permute-start.10) | collective-permute-done | bytes 262176 | tf_op jit(solution)/shard_map/ppermute | solution.py:90
  278.0 0.7 bitcast_dynamic-update-slice_fusion.4
  278.8 4.9 %collective-permute-done.11 = bf16[1,64,2048]{2,1,0:T(8,128)(2,1)S(1)} collective-permute-done((bf16[1,64,2048]{2,1,0:T(8,128)(2,1)S(1)}, bf16[1,64,2048]{2,1,0:T(8,128)(2,1)S(1)}, u32[]{:S(2)}, u32[]{:S(2)}) %collective-permute-start.11) | collective-permute-done | bytes 262176 | tf_op jit(solution)/shard_map/ppermute | solution.py:90
  283.6 0.7 bitcast_dynamic-update-slice_fusion.3
  284.4 4.9 %collective-permute-done.12 = bf16[1,64,2048]{2,1,0:T(8,128)(2,1)S(1)} collective-permute-done((bf16[1,64,2048]{2,1,0:T(8,128)(2,1)S(1)}, bf16[1,64,2048]{2,1,0:T(8,128)(2,1)S(1)}, u32[]{:S(2)}, u32[]{:S(2)}) %collective-permute-start.12) | collective-permute-done | bytes 262176 | tf_op jit(solution)/shard_map/ppermute | solution.py:90
  289.3 0.7 bitcast_dynamic-update-slice_fusion.2
  290.0 5.9 %collective-permute-done.13 = bf16[1,64,2048]{2,1,0:T(8,128)(2,1)S(1)} collective-permute-done((bf16[1,64,2048]{2,1,0:T(8,128)(2,1)S(1)}, bf16[1,64,2048]{2,1,0:T(8,128)(2,1)S(1)}, u32[]{:S(2)}, u32[]{:S(2)}) %collective-permute-start.13) | collective-permute-done | bytes 262176 | tf_op jit(solution)/shard_map/ppermute | solution.py:90
  295.9 0.7 bitcast_dynamic-update-slice_fusion.1
  296.6 3.9 %collective-permute-done.14 = bf16[1,64,2048]{2,1,0:T(8,128)(2,1)S(1)} collective-permute-done((bf16[1,64,2048]{2,1,0:T(8,128)(2,1)S(1)}, bf16[1,64,2048]{2,1,0:T(8,128)(2,1)S(1)}, u32[]{:S(2)}, u32[]{:S(2)}) %collective-permute-start.14) | collective-permute-done | bytes 262176 | tf_op jit(solution)/shard_map/ppermute | solution.py:90
  300.5 0.7 bitcast_dynamic-update-slice_fusion
  301.3 5.0 %gather_fusion.3 = bf16[16,64,2048]{2,1,0:T(8,128)(2,1)} fusion(bf16[16,64,2048]{2,1,0:T(8,128)(2,1)} %bitcast.143, s32[1024]{0:T(1024)S(1)} %pad_clamp_fusion.1), kind=kCustom, calls=%fused_computation.3 | custom fusion | bytes 8388672 | tf_op jit(solution)/shard_map/gather | solution.py:92
  306.2 7.1 %gather_fusion.4 = bf16[512,2048]{1,0:T(8,128)(2,1)S(1)} fusion(bf16[1024,2048]{1,0:T(8,128)(2,1)} %bitcast.140, s32[1024]{0:T(1024)S(1)} %get-tuple-element.121), kind=kCustom, calls=%fused_computation.4 | custom fusion | bytes 4196352 | tf_op jit(solution)/shard_map/gather | solution.py:96
  313.4 2.5 fusion.12
  (57 shorter events, 2.1 us)
Async XLA Ops:
  0.0 15.9 %copy-start = (bf16[64,2048]{1,0:T(8,128)(2,1)S(1)}, bf16[64,2048]{1,0:T(8,128)(2,1)}, u32[]{:S(2)}) copy-start(bf16[64,2048]{1,0:T(8,128)(2,1)} %param.8) | copy-start | bytes 786436
  6.8 19.6 %all-to-all-start = ((bf16[16,1,1]{2,1,0:T(2,128)(2,1)}), bf16[16,1,1]{2,1,0:T(2,128)(2,1)S(1)}, u32[]{:S(2)}, u32[]{:S(2)}) async-start(bf16[16,1,1]{2,1,0:T(2,128)(2,1)} %copy.33), calls=%async_computation | async-start | bytes 16384 | tf_op jit(solution)/shard_map/all_to_all | solution.py:54
  26.4 98.5 %all-to-all-start.1 = ((bf16[16,64,2048]{2,1,0:T(8,128)(2,1)}), bf16[16,64,2048]{2,1,0:T(8,128)(2,1)}, u32[]{:S(2)}, u32[]{:S(2)}) async-start(bf16[16,64,2048]{2,1,0:T(8,128)(2,1)} %broadcast_select_fusion), calls=%async_computation.1 | async-start | bytes 8388608 | tf_op jit(solution)/shard_map/all_to_all | solution.py:53
  141.1 2.9 copy-start.2
  177.5 1.4 copy-start.1
  178.8 5.5 %collective-permute-start = (bf16[1,64,2048]{2,1,0:T(8,128)(2,1)}, bf16[1,64,2048]{2,1,0:T(8,128)(2,1)}, u32[]{:S(2)}, u32[]{:S(2)}) collective-permute-start(bf16[1,64,2048]{2,1,0:T(8,128)(2,1)} %get-tuple-element.74), channel_id=1, source_target_pairs={{0,1},{1,0},{2,3},{3,2},{4,5},{5,4},{6,7},{7,6},{8,9},{9,8},{10,11... | collective-permute-start | bytes 786440 | tf_op jit(solution)/shard_map/ppermute | solution.py:90
  179.0 9.8 %collective-permute-start.1 = (bf16[1,64,2048]{2,1,0:T(8,128)(2,1)}, bf16[1,64,2048]{2,1,0:T(8,128)(2,1)S(1)}, u32[]{:S(2)}, u32[]{:S(2)}) collective-permute-start(bf16[1,64,2048]{2,1,0:T(8,128)(2,1)} %get-tuple-element.73), channel_id=1, source_target_pairs={{0,2},{1,3},{2,0},{3,1},{4,6},{5,7},{6,4},{7,5},{8,10},{9,11},{10,... | collective-permute-start | bytes 786440 | tf_op jit(solution)/shard_map/ppermute | solution.py:90
  179.1 14.5 %collective-permute-start.2 = (bf16[1,64,2048]{2,1,0:T(8,128)(2,1)}, bf16[1,64,2048]{2,1,0:T(8,128)(2,1)S(1)}, u32[]{:S(2)}, u32[]{:S(2)}) collective-permute-start(bf16[1,64,2048]{2,1,0:T(8,128)(2,1)} %get-tuple-element.72), channel_id=1, source_target_pairs={{0,3},{1,2},{2,1},{3,0},{4,7},{5,6},{6,5},{7,4},{8,11},{9,10},{10,... | collective-permute-start | bytes 786440 | tf_op jit(solution)/shard_map/ppermute | solution.py:90
  181.1 33.3 %collective-permute-start.3 = (bf16[1,64,2048]{2,1,0:T(8,128)(2,1)S(1)}, bf16[1,64,2048]{2,1,0:T(8,128)(2,1)S(1)}, u32[]{:S(2)}, u32[]{:S(2)}) collective-permute-start(bf16[1,64,2048]{2,1,0:T(8,128)(2,1)S(1)} %get-tuple-element.71), channel_id=1, source_target_pairs={{0,4},{1,5},{2,6},{3,7},{4,0},{5,1},{6,2},{7,3},{8,12},{9,13},{10,... | collective-permute-start | bytes 786440 | tf_op jit(solution)/shard_map/ppermute | solution.py:90
  183.9 31.2 %collective-permute-start.4 = (bf16[1,64,2048]{2,1,0:T(8,128)(2,1)S(1)}, bf16[1,64,2048]{2,1,0:T(8,128)(2,1)S(1)}, u32[]{:S(2)}, u32[]{:S(2)}) collective-permute-start(bf16[1,64,2048]{2,1,0:T(8,128)(2,1)S(1)} %get-tuple-element.70), channel_id=1, source_target_pairs={{0,5},{1,4},{2,7},{3,6},{4,1},{5,0},{6,3},{7,2},{8,13},{9,12},{10,... | collective-permute-start | bytes 786440 | tf_op jit(solution)/shard_map/ppermute | solution.py:90
  184.3 34.1 %collective-permute-start.5 = (bf16[1,64,2048]{2,1,0:T(8,128)(2,1)S(1)}, bf16[1,64,2048]{2,1,0:T(8,128)(2,1)S(1)}, u32[]{:S(2)}, u32[]{:S(2)}) collective-permute-start(bf16[1,64,2048]{2,1,0:T(8,128)(2,1)S(1)} %get-tuple-element.69), channel_id=1, source_target_pairs={{0,6},{1,7},{2,4},{3,5},{4,2},{5,3},{6,0},{7,1},{8,14},{9,15},{10,... | collective-permute-start | bytes 786440 | tf_op jit(solution)/shard_map/ppermute | solution.py:90
  188.8 34.6 %collective-permute-start.6 = (bf16[1,64,2048]{2,1,0:T(8,128)(2,1)S(1)}, bf16[1,64,2048]{2,1,0:T(8,128)(2,1)S(1)}, u32[]{:S(2)}, u32[]{:S(2)}) collective-permute-start(bf16[1,64,2048]{2,1,0:T(8,128)(2,1)S(1)} %get-tuple-element.68), channel_id=1, source_target_pairs={{0,7},{1,6},{2,5},{3,4},{4,3},{5,2},{6,1},{7,0},{8,15},{9,14},{10,... | collective-permute-start | bytes 786440 | tf_op jit(solution)/shard_map/ppermute | solution.py:90
  193.6 50.7 %collective-permute-start.7 = (bf16[1,64,2048]{2,1,0:T(8,128)(2,1)S(1)}, bf16[1,64,2048]{2,1,0:T(8,128)(2,1)S(1)}, u32[]{:S(2)}, u32[]{:S(2)}) collective-permute-start(bf16[1,64,2048]{2,1,0:T(8,128)(2,1)S(1)} %get-tuple-element.67), channel_id=1, source_target_pairs={{0,8},{1,9},{2,10},{3,11},{4,12},{5,13},{6,14},{7,15},{8,0},{9,1},... | collective-permute-start | bytes 786440 | tf_op jit(solution)/shard_map/ppermute | solution.py:90
  214.4 41.0 %collective-permute-start.8 = (bf16[1,64,2048]{2,1,0:T(8,128)(2,1)S(1)}, bf16[1,64,2048]{2,1,0:T(8,128)(2,1)S(1)}, u32[]{:S(2)}, u32[]{:S(2)}) collective-permute-start(bf16[1,64,2048]{2,1,0:T(8,128)(2,1)S(1)} %get-tuple-element.66), channel_id=1, source_target_pairs={{0,9},{1,8},{2,11},{3,10},{4,13},{5,12},{6,15},{7,14},{8,1},{9,0},... | collective-permute-start | bytes 786440 | tf_op jit(solution)/shard_map/ppermute | solution.py:90
  215.1 46.0 %collective-permute-start.9 = (bf16[1,64,2048]{2,1,0:T(8,128)(2,1)S(1)}, bf16[1,64,2048]{2,1,0:T(8,128)(2,1)S(1)}, u32[]{:S(2)}, u32[]{:S(2)}) collective-permute-start(bf16[1,64,2048]{2,1,0:T(8,128)(2,1)S(1)} %get-tuple-element.65), channel_id=1, source_target_pairs={{0,10},{1,11},{2,8},{3,9},{4,14},{5,15},{6,12},{7,13},{8,2},{9,3},... | collective-permute-start | bytes 786440 | tf_op jit(solution)/shard_map/ppermute | solution.py:90
  218.3 59.7 %collective-permute-start.10 = (bf16[1,64,2048]{2,1,0:T(8,128)(2,1)S(1)}, bf16[1,64,2048]{2,1,0:T(8,128)(2,1)S(1)}, u32[]{:S(2)}, u32[]{:S(2)}) collective-permute-start(bf16[1,64,2048]{2,1,0:T(8,128)(2,1)S(1)} %get-tuple-element.64), channel_id=1, source_target_pairs={{0,11},{1,10},{2,9},{3,8},{4,15},{5,14},{6,13},{7,12},{8,3},{9,2},... | collective-permute-start | bytes 786440 | tf_op jit(solution)/shard_map/ppermute | solution.py:90
  223.4 60.2 %collective-permute-start.11 = (bf16[1,64,2048]{2,1,0:T(8,128)(2,1)S(1)}, bf16[1,64,2048]{2,1,0:T(8,128)(2,1)S(1)}, u32[]{:S(2)}, u32[]{:S(2)}) collective-permute-start(bf16[1,64,2048]{2,1,0:T(8,128)(2,1)S(1)} %get-tuple-element.63), channel_id=1, source_target_pairs={{0,12},{1,13},{2,14},{3,15},{4,8},{5,9},{6,10},{7,11},{8,4},{9,5},... | collective-permute-start | bytes 786440 | tf_op jit(solution)/shard_map/ppermute | solution.py:90
  244.3 44.9 %collective-permute-start.12 = (bf16[1,64,2048]{2,1,0:T(8,128)(2,1)S(1)}, bf16[1,64,2048]{2,1,0:T(8,128)(2,1)S(1)}, u32[]{:S(2)}, u32[]{:S(2)}) collective-permute-start(bf16[1,64,2048]{2,1,0:T(8,128)(2,1)S(1)} %get-tuple-element.62), channel_id=1, source_target_pairs={{0,13},{1,12},{2,15},{3,14},{4,9},{5,8},{6,11},{7,10},{8,5},{9,4},... | collective-permute-start | bytes 786440 | tf_op jit(solution)/shard_map/ppermute | solution.py:90
  255.4 40.5 %collective-permute-start.13 = (bf16[1,64,2048]{2,1,0:T(8,128)(2,1)S(1)}, bf16[1,64,2048]{2,1,0:T(8,128)(2,1)S(1)}, u32[]{:S(2)}, u32[]{:S(2)}) collective-permute-start(bf16[1,64,2048]{2,1,0:T(8,128)(2,1)S(1)} %get-tuple-element.61), channel_id=1, source_target_pairs={{0,14},{1,15},{2,12},{3,13},{4,10},{5,11},{6,8},{7,9},{8,6},{9,7},... | collective-permute-start | bytes 786440 | tf_op jit(solution)/shard_map/ppermute | solution.py:90
  261.2 39.4 %collective-permute-start.14 = (bf16[1,64,2048]{2,1,0:T(8,128)(2,1)S(1)}, bf16[1,64,2048]{2,1,0:T(8,128)(2,1)S(1)}, u32[]{:S(2)}, u32[]{:S(2)}) collective-permute-start(bf16[1,64,2048]{2,1,0:T(8,128)(2,1)S(1)} %get-tuple-element.60), channel_id=1, source_target_pairs={{0,15},{1,14},{2,13},{3,12},{4,11},{5,10},{6,9},{7,8},{8,7},{9,6},... | collective-permute-start | bytes 786440 | tf_op jit(solution)/shard_map/ppermute | solution.py:90
